TPU v7x, 128 devices: a whole 4x4x4 slice. The times are simulated.
128 devices in a mesh: fsdp: 128 (over y, z, x, core).
Axes of the slice: x: 4, y: 4, z: 4, core: 2. Of those that a mesh axis runs over, the one named last changes fastest.
Arguments:
- hidden_in: bfloat16 [16384, 1024], P('fsdp'), may hold values from -24 to 24
- norm1_gain: bfloat16 [1024], P('fsdp'), may hold values from 0.099609375 to 1.8984375
- in_weight: bfloat16 [1024, 3072], P('fsdp'), may hold values from -0.1875 to 0.1875
- conv_weight: bfloat16 [1024, 3], P('fsdp'), may hold values from -3 to 3
- out_weight: bfloat16 [1024, 1024], P('fsdp'), may hold values from -0.1875 to 0.1875
- norm2_gain: bfloat16 [1024], P('fsdp'), may hold values from 0.099609375 to 1.8984375
- gate_weight: bfloat16 [1024, 4608], P('fsdp'), may hold values from -0.1875 to 0.1875
- up_weight: bfloat16 [1024, 4608], P('fsdp'), may hold values from -0.1875 to 0.1875
- down_weight: bfloat16 [4608, 1024], P('fsdp'), may hold values from -0.125 to 0.125
- segment_ids: int32 [16384], P('fsdp'), may hold values from 0 to 63, never falling along the last dimension, each value on 1 to 512 neighbouring positions
- cotangent: bfloat16 [16384, 1024], P('fsdp'), may hold values from -6 to 6
Outputs:
- block_out: bfloat16 [16384, 1024], P('fsdp')
- input_grad: float32 [16384, 1024], P('fsdp')
- norm1_gain_grad: float32 [1024], P('fsdp')
- in_weight_grad: float32 [1024, 3072], P('fsdp')
- conv_weight_grad: float32 [1024, 3], P('fsdp')
- out_weight_grad: float32 [1024, 1024], P('fsdp')
- norm2_gain_grad: float32 [1024], P('fsdp')
- gate_weight_grad: float32 [1024, 4608], P('fsdp')
- up_weight_grad: float32 [1024, 4608], P('fsdp')
- down_weight_grad: float32 [4608, 1024], P('fsdp')
Inputs may be any that keep to these rules, and one draw needn't show every extreme that they name: `segment_ids`: document numbers never fall along the tokens; each document covers 1 to 512 tokens, one exactly 512.
All inputs are finite; a program needn't handle non-finite values.
Results may differ from a plain program's by a relative error of at most 0.011.
Values may be sent and summed in bfloat16 or wider, within the bound.
A program may use at most 192 MiB of HBM per device.

v0:
```python
import jax
import jax.numpy as jnp
from jax import lax
from jax.sharding import PartitionSpec as P

CONV = 3
EPS = 1e-05
LANE = 256


def shifted(value, axis, by):
    size = lax.axis_size(axis)
    pairs = [(i, i + by) for i in range(size) if 0 <= i + by < size]
    return lax.ppermute(value, axis, pairs)


def rms_scale(values):
    return lax.rsqrt(jnp.mean(values * values, axis=-1, keepdims=True) + EPS)


def pad_cols(x):
    extra = -x.shape[1] % LANE
    return jnp.pad(x, ((0, 0), (0, extra))) if extra else x


def gather_packed(pieces):
    widths = [p.shape[1] for p in pieces]
    packed = jnp.concatenate(pieces, axis=1)
    full = lax.all_gather(packed, "fsdp", axis=0, tiled=True)
    out, at = ([], 0)
    for w in widths:
        out.append(full[:, at : at + w])
        at += w
    return out


def scatter_packed(pieces):
    widths = [p.shape[1] for p in pieces]
    packed = jnp.concatenate(pieces, axis=1)
    mine = lax.optimization_barrier(
        lax.psum_scatter(packed, "fsdp", scatter_dimension=0, tiled=True)
    )
    out, at = ([], 0)
    for w in widths:
        out.append(mine[:, at : at + w])
        at += w
    return out


def per_device(
    hidden_in,
    norm1_gain,
    in_weight,
    conv_weight,
    out_weight,
    norm2_gain,
    gate_weight,
    up_weight,
    down_weight,
    segment_ids,
    cotangent,
):
    rows = hidden_in.shape[0]
    width = hidden_in.shape[1]
    per = in_weight.shape[0]
    n = lax.axis_size("fsdp")
    down_rows = down_weight.shape[0]
    small = jnp.concatenate([norm1_gain[:, None], norm2_gain[:, None], conv_weight], axis=1)
    n_small = small.shape[1]
    w_in, w_out, small_full = gather_packed([in_weight, out_weight, pad_cols(small)])
    w_gate, w_up, w_down_packed = gather_packed(
        [gate_weight, up_weight, down_weight.reshape(per, -1)]
    )
    w_down = w_down_packed.reshape(n * down_rows, width)
    gain1 = small_full[:, 0]
    gain2 = small_full[:, 1]
    w_conv = small_full[:, 2 : 2 + CONV]
    xf = hidden_in.astype(jnp.float32)
    s1 = rms_scale(xf)
    h = (xf * s1 * gain1.astype(jnp.float32)).astype(jnp.bfloat16)
    proj = jnp.dot(h, w_in, preferred_element_type=jnp.float32)
    bgate = proj[:, :width]
    cgate = proj[:, width : 2 * width]
    xv = proj[:, 2 * width :]
    bx = (bgate * xv).astype(jnp.bfloat16)
    prev_rows, prev_ids = shifted(
        (bx[rows - 2 :], segment_ids[rows - 2 :].astype(jnp.bfloat16)), "fsdp", 1
    )
    ext_bx = jnp.concatenate([prev_rows, bx], axis=0).astype(jnp.float32)
    ext_ids = jnp.concatenate([prev_ids.astype(jnp.int32), segment_ids], axis=0)
    taps = w_conv.astype(jnp.float32)
    masks = [
        (ext_ids[2 - k : 2 - k + rows] == segment_ids).astype(jnp.float32)[:, None]
        for k in range(CONV)
    ]
    conv_out = jnp.zeros((rows, width), jnp.float32)
    for k in range(CONV):
        conv_out = conv_out + taps[:, k] * masks[k] * ext_bx[2 - k : 2 - k + rows]
    y = (cgate * conv_out).astype(jnp.bfloat16)
    resid = xf + jnp.dot(y, w_out, preferred_element_type=jnp.float32)
    s2 = rms_scale(resid)
    gain2f = gain2.astype(jnp.float32)
    h2 = (resid * s2 * gain2f).astype(jnp.bfloat16)
    a = jnp.dot(h2, w_gate, preferred_element_type=jnp.float32)
    b = jnp.dot(h2, w_up, preferred_element_type=jnp.float32)
    sig = jax.nn.sigmoid(a)
    act = a * sig
    z = (act * b).astype(jnp.bfloat16)
    block_out = (resid + jnp.dot(z, w_down, preferred_element_type=jnp.float32)).astype(
        jnp.bfloat16
    )
    dz = lax.dot_general(
        cotangent, w_down, (((1,), (1,)), ((), ())), preferred_element_type=jnp.float32
    )
    da = (dz * b * sig * (1.0 + a * (1.0 - sig))).astype(jnp.bfloat16)
    db = (dz * act).astype(jnp.bfloat16)
    g_down = lax.dot_general(
        z, cotangent, (((0,), (0,)), ((), ())), preferred_element_type=jnp.float32
    )
    g_gate = lax.dot_general(h2, da, (((0,), (0,)), ((), ())), preferred_element_type=jnp.float32)
    g_up = lax.dot_general(h2, db, (((0,), (0,)), ((), ())), preferred_element_type=jnp.float32)
    own_gate, own_up, own_down = scatter_packed([g_gate, g_up, g_down.reshape(n * per, -1)])
    dh2 = lax.dot_general(da, w_gate, (((1,), (1,)), ((), ())), preferred_element_type=jnp.float32)
    dh2 = dh2 + lax.dot_general(
        db, w_up, (((1,), (1,)), ((), ())), preferred_element_type=jnp.float32
    )
    g_gain2 = jnp.sum(dh2 * resid * s2, axis=0)
    dn2 = dh2 * gain2f
    d_resid = (
        cotangent.astype(jnp.float32)
        + s2 * dn2
        - resid * (s2 * s2 * s2) * jnp.mean(dn2 * resid, axis=-1, keepdims=True)
    )
    d_out = d_resid.astype(jnp.bfloat16)
    g_out = lax.dot_general(y, d_out, (((0,), (0,)), ((), ())), preferred_element_type=jnp.float32)
    dy = lax.dot_general(d_out, w_out, (((1,), (1,)), ((), ())), preferred_element_type=jnp.float32)
    d_cgate = dy * conv_out
    d_conv = dy * cgate
    d_ext = jnp.zeros((rows + 2, width), jnp.float32)
    tap_cols = []
    for k in range(CONV):
        term = d_conv * masks[k]
        d_ext = d_ext + jnp.pad(taps[:, k] * term, ((2 - k, k), (0, 0)))
        tap_cols.append(jnp.sum(term * ext_bx[2 - k : 2 - k + rows], axis=0))
    g_conv = jnp.stack(tap_cols, axis=1)
    returned = shifted(d_ext[:2], "fsdp", -1)
    d_bx = d_ext[2:] + jnp.pad(returned, ((rows - 2, 0), (0, 0)))
    d_proj = jnp.concatenate([d_bx * xv, d_cgate, d_bx * bgate], axis=1).astype(jnp.bfloat16)
    g_in = lax.dot_general(h, d_proj, (((0,), (0,)), ((), ())), preferred_element_type=jnp.float32)
    dh = lax.dot_general(d_proj, w_in, (((1,), (1,)), ((), ())), preferred_element_type=jnp.float32)
    g_gain1 = jnp.sum(dh * xf * s1, axis=0)
    dn1 = dh * gain1.astype(jnp.float32)
    input_grad = (
        d_resid + s1 * dn1 - xf * (s1 * s1 * s1) * jnp.mean(dn1 * xf, axis=-1, keepdims=True)
    )
    g_small = jnp.concatenate([g_gain1[:, None], g_gain2[:, None], g_conv], axis=1)
    own_in, own_out, own_small = scatter_packed([g_in, g_out, pad_cols(g_small)])
    return (
        block_out,
        input_grad,
        own_small[:, 0],
        own_in,
        own_small[:, 2 : 2 + CONV],
        own_out,
        own_small[:, 1],
        own_gate,
        own_up,
        own_down.reshape(down_rows, width),
    )


def solution(mesh):
    return jax.shard_map(
        per_device,
        mesh=mesh,
        in_specs=(
            P("fsdp", None),
            P("fsdp"),
            P("fsdp", None),
            P("fsdp", None),
            P("fsdp", None),
            P("fsdp"),
            P("fsdp", None),
            P("fsdp", None),
            P("fsdp", None),
            P("fsdp"),
            P("fsdp", None),
        ),
        out_specs=(
            P("fsdp", None),
            P("fsdp", None),
            P("fsdp"),
            P("fsdp", None),
            P("fsdp", None),
            P("fsdp", None),
            P("fsdp"),
            P("fsdp", None),
            P("fsdp", None),
            P("fsdp", None),
        ),
        check_vma=False,
    )
```

profile of v0, /device:TPU:0, one launch (start us, length us, event | category | flops | bytes accessed | tf_op | source)
XLA Modules:
  0.0 1274.9 jit_solution(17129408030517518262)
XLA Ops:
  7.2 0.0 all-gather.3.cloned.1.call-start
  7.2 0.7 pad_maximum_fusion.5
  7.9 0.1 copy.41
  8.0 1.5 fusion.39
  9.5 0.0 all-gather.5.cloned.1.call-start
  9.6 1.0 reshape.87
  10.6 1.6 pad_maximum_fusion.4
  12.2 0.0 reduce-scatter.3.cloned.1.call-start
  12.2 0.7 convert.14
  12.9 0.1 slice.118
  13.0 1.3 collective-permute-start.1
  14.3 1.1 fusion.24
  15.4 0.5 multiply_multiply_fusion.2
  15.9 0.7 pad_add_fusion.2
  16.6 0.7 compare_convert_fusion.1
  17.4 67.1 %all-gather.3.cloned.1.call-done = bf16[1024,4352]{1,0:T(8,128)(2,1)} async-done(((bf16[8,4352]{1,0:T(8,128)(2,1)}), bf16[1024,4352]{1,0:T(8,128)(2,1)}) %all-gather.3.cloned.1.call-update) | async-done | bytes 8912912 | tf_op jit(solution)/shard_map/all_gather | solution.py:29
  84.5 1.4 convert_reduce_fusion
  85.9 4.0 fusion.10
  89.9 0.1 multiply_convert_fusion.8
  89.9 2.2 collective-permute-start
  92.1 1.1 slice_convert_fusion
  93.2 0.8 slice_reduce_fusion.2
  94.0 0.1 maximum_convert_fusion
  94.1 1.1 multiply_convert_fusion.7
  95.2 2.3 multiply_reduce_fusion.5
  97.5 0.1 multiply_convert_fusion.6
  97.6 85.5 %all-gather.5.cloned.1.call-done = bf16[1024,13824]{1,0:T(8,128)(2,1)} async-done(((bf16[8,13824]{1,0:T(8,128)(2,1)}), bf16[1024,13824]{1,0:T(8,128)(2,1)}) %all-gather.5.cloned.1.call-update) | async-done | bytes 28311568 | tf_op jit(solution)/shard_map/all_gather | solution.py:29
  183.1 7.9 slice.156
  191.1 17.4 %reshape.88 = bf16[4608,1024]{1,0:T(8,128)(2,1)} reshape(bf16[1024,4608]{1,0:T(8,128)(2,1)} %slice.156) | data formatting | bytes 18874368 | tf_op jit(solution)/shard_map/reshape | solution.py:74
  208.5 6.9 convolution_bitcast_fusion
  215.4 5.1 fusion.2
  220.5 5.8 multiply_convert_fusion.1
  226.3 7.6 fusion
  234.0 6.0 multiply_reduce_fusion.3
  240.1 0.2 multiply_subtract_fusion
  240.3 2.7 fusion.34
  243.0 0.8 fusion.13
  243.9 0.3 multiply_reduce_fusion
  244.2 0.2 broadcast_multiply_fusion
  244.4 1.5 collective-permute-start.2
  245.8 0.1 pad_add_fusion
  246.0 1.6 collective-permute-done.2
  247.6 0.2 multiply_convert_fusion.5
  247.8 6.5 fusion.32
  254.2 3.0 fusion.31
  257.3 0.2 copy.36
  257.5 11.7 select_maximum_fusion
  269.2 0.0 reduce-scatter.5.cloned.1.call-start
  269.2 7.9 fusion.45
  277.2 21.6 %reshape.89 = f32[1024,4608]{1,0:T(8,128)} reshape(f32[4608,1024]{1,0:T(8,128)} %fusion.45) | data formatting | bytes 37748736 | tf_op jit(solution)/shard_map/reshape | solution.py:122
  298.8 9.3 fusion.43
  308.1 7.9 fusion.44
  316.0 37.7 %pad_maximum_fusion = f32[1024,13824]{1,0:T(8,128)} fusion(f32[1024,4608]{1,0:T(8,128)} %reshape.89, f32[1024,4608]{1,0:T(8,128)} %fusion.44, f32[1024,4608]{1,0:T(8,128)} %fusion.43), kind=kLoop, calls=%fused_computation | loop fusion | flops 28311552 | bytes 113246208 | tf_op jit(solution)/shard_map/concatenate | solution.py:39
  353.7 5.9 fusion.23
  359.7 1.0 fusion.28
  360.7 582.3 %reduce-scatter.3.cloned.1.call-done = f32[8,4352]{1,0:T(8,128)} async-done(((f32[1024,4352]{1,0:T(8,128)}), f32[8,4352]{1,0:T(8,128)}) %reduce-scatter.3.cloned.1.call-update) | async-done | bytes 139280 | tf_op jit(solution)/shard_map/reduce_scatter | solution.py:41
  942.9 0.8 slice.160
  943.7 1.4 slice.161
  945.0 1.5 slice.159
  946.6 0.7 copy.38
  947.2 1.5 slice_reduce_fusion.3
  948.7 317.1 %reduce-scatter.5.cloned.1.call-done = f32[8,13824]{1,0:T(8,128)} async-done(((f32[1024,13824]{1,0:T(8,128)}), f32[8,13824]{1,0:T(8,128)}) %reduce-scatter.5.cloned.1.call-update) | async-done | bytes 442384 | tf_op jit(solution)/shard_map/reduce_scatter | solution.py:41
  1265.8 1.8 fusion.42
  1267.6 0.7 reshape.90
  (48 shorter events, 0.2 us)
Async XLA Ops:
  7.2 77.3 %all-gather.3.cloned.1.call-start = ((), (), s32[]{:S(2)}) async-start(), calls=%async_computation.2 | async-start | bytes 8982528 | tf_op jit(solution)/shard_map/all_gather | solution.py:29
  9.5 173.6 %all-gather.5.cloned.1.call-start = ((), (), s32[]{:S(2)}) async-start(), calls=%async_computation.3 | async-start | bytes 28532736 | tf_op jit(solution)/shard_map/all_gather | solution.py:29
  12.2 930.7 %reduce-scatter.3.cloned.1.call-start = ((), (), s32[]{:S(2)}) async-start(), calls=%async_computation.4 | async-start | bytes 17965056 | tf_op jit(solution)/shard_map/reduce_scatter | solution.py:41
  13.0 2.9 collective-permute-start.1
  85.9 9.3 copy-start.3
  89.9 4.2 copy-start
  89.9 4.0 collective-permute-start
  95.2 95.9 %copy-start.10 = (bf16[128,1024]{1,0:T(8,128)(2,1)}, bf16[128,1024]{1,0:T(8,128)(2,1)S(1)}, u32[]{:S(2)}) copy-start(bf16[128,1024]{1,0:T(8,128)(2,1)S(1)} %get-tuple-element.55) | copy-start | bytes 786436
  191.1 17.4 %copy-start.2 = (bf16[128,1024]{1,0:T(8,128)(2,1)S(1)}, bf16[128,1024]{1,0:T(8,128)(2,1)}, u32[]{:S(2)}) copy-start(bf16[128,1024]{1,0:T(8,128)(2,1)} %param.21) | copy-start | bytes 786436
  226.3 7.6 copy-start.7
  226.3 7.7 copy-start.9
  233.9 9.1 slice-start
  234.0 6.3 copy-start.11
  234.0 9.0 slice-start.1
  234.0 9.0 slice-start.2
  240.1 3.8 copy-start.1
  240.1 3.8 copy-start.6
  243.8 3.9 copy-start.4
  244.4 3.2 collective-permute-start.2
  269.2 996.6 %reduce-scatter.5.cloned.1.call-start = ((), (), s32[]{:S(2)}) async-start(), calls=%async_computation.5 | async-start | bytes 57065472 | tf_op jit(solution)/shard_map/reduce_scatter | solution.py:41
  298.8 9.3 copy-start.8
  353.7 6.0 copy-start.5
  353.7 5.9 copy-start.12
  353.7 5.9 copy-start.13
Sparse Core Ops, SparseCore 0:
  11.5 72.8 all-gather.2
  87.5 95.5 all-gather.4
  269.3 673.5 reduce-scatter.2
  949.2 316.6 reduce-scatter.4
where the time goes:
time: 1280 us; the launch traced here: 1270 us
  waiting for transfers between devices  1050 us (82%)
  matrix products  81.7 us (6%)
  other arithmetic  62.7 us (5%)
  local copies, waits for them, and re-layouts  57.6 us (4%)
  between operations  14.2 us (1%)
    reduce_scatter x2, waiting for transfers between devices, scatter_packed(): lax.psum_scatter(packed, 'fsdp', scatter_dimension=0, tiled=True)  899 us
    all_gather x2, waiting for transfers between devices, gather_packed(): full = lax.all_gather(packed, 'fsdp', axis=0, tiled=True)  153 us
    concatenate x2, other arithmetic, scatter_packed(): packed = jnp.concatenate(pieces, axis=1)  49.4 us
  transfers between devices with their start and end apart: 7, of which 5 were waited for; matrix products, arithmetic and copies ran while one was open for 9% of the time, Pallas kernels for 0%

commit v1 on v0

--- a/solution.py
+++ b/solution.py
@@ -26,7 +26,17 @@
 def gather_packed(pieces):
     widths = [p.shape[1] for p in pieces]
     packed = jnp.concatenate(pieces, axis=1)
-    full = lax.all_gather(packed, "fsdp", axis=0, tiled=True)
+
+    def attach_axis_part(my_tile):
+        fields = []
+        for _ in range(jax.lax.psum(1, axis_name="fsdp")):
+            fields.append(my_tile)
+        return jnp.concatenate(
+            jax.lax.all_to_all(jnp.stack(fields), split_axis=0, concat_axis=0, axis_name="fsdp"),
+            axis=0,
+        )
+
+    full = attach_axis_part(packed)
     out, at = ([], 0)
     for w in widths:
         out.append(full[:, at : at + w])

time: 1280 us -> 1700 us (1.33)
  starting transfers between devices: 5.07 us -> 449 us
  waiting for transfers between devices: 1050 us -> 1020 us
    ppermute x3, starting transfers between devices: 4.91 us -> 422 us  [shifted(): return lax.ppermute(value, axis, pairs)]
    all_gather x2 -> x0, waiting for transfers between devices: 153 us -> none  [gather_packed(): full = lax.all_gather(packed, 'fsdp', axis=0, tiled=True)]
    all_to_all x0 -> x2, waiting for transfers between devices: none -> 106 us  [attach_axis_part(): jax.lax.all_to_all(jnp.stack(fields), split_axis=0, concat_axis=0, axis_n...]
    all_to_all x0 -> x2, starting transfers between devices: none -> 27 us  [attach_axis_part(): jax.lax.all_to_all(jnp.stack(fields), split_axis=0, concat_axis=0, axis_n...]
  transfers between devices with their start and end apart: 7 -> 7, of which waited for: 5 -> 5; matrix products, arithmetic and copies ran while one was open for 9% -> 6% of each run, Pallas kernels for 0% -> 0%
where the time goes in v1:
time: 1700 us
  waiting for transfers between devices  1020 us (60%)
  starting transfers between devices  449 us (26%)
  matrix products  87.4 us (5%)
  local copies, waits for them, and re-layouts  70.2 us (4%)
  other arithmetic  57.5 us (3%)
    reduce_scatter x2, waiting for transfers between devices, scatter_packed(): lax.psum_scatter(packed, 'fsdp', scatter_dimension=0, tiled=True)  909 us
    ppermute x3, starting transfers between devices, shifted(): return lax.ppermute(value, axis, pairs)  422 us
    all_to_all x2, waiting for transfers between devices, attach_axis_part(): jax.lax.all_to_all(jnp.stack(fields), split_axis=0, concat_axis=0, axis_n...  106 us
    concatenate x2, other arithmetic, scatter_packed(): packed = jnp.concatenate(pieces, axis=1)  49.4 us
  transfers between devices with their start and end apart: 7, of which 5 were waited for; matrix products, arithmetic and copies ran while one was open for 6% of the time, Pallas kernels for 0%

profile of v1, /device:TPU:0, one launch (start us, length us, event | category | flops | bytes accessed | tf_op | source)
XLA Modules:
  0.0 1696.6 jit_solution(17517105492101904245)
XLA Ops:
  7.2 0.7 pad_maximum_fusion.5
  7.9 0.1 copy.51
  8.0 0.8 fusion.39
  8.8 4.0 stack.10
  12.8 11.6 all-to-all-start
  24.4 0.1 reshape.98
  24.6 106.2 %all-to-all-done = bf16[128,8,4352]{2,1,0:T(8,128)(2,1)} async-done(((bf16[128,8,4352]{2,1,0:T(8,128)(2,1)}), bf16[128,8,4352]{2,1,0:T(8,128)(2,1)}, u32[]{:S(2)}, u32[]{:S(2)}) %all-to-all-start) | async-done | bytes 8912928 | tf_op jit(solution)/shard_map/all_to_all | solution.py:35
  130.8 9.5 stack.11
  140.4 15.4 all-to-all-start.1
  155.7 0.0 reduce-scatter.3.cloned.1.call-start
  155.8 0.1 slice.118
  155.9 1.3 collective-permute-start.1
  157.2 0.1 fusion.24
  157.3 0.5 multiply_multiply_fusion.2
  157.8 0.1 collective-permute-done.1
  158.0 0.1 pad_add_fusion.2
  158.1 0.1 compare_convert_fusion.1
  158.1 1.3 convert_reduce_fusion
  159.5 3.8 fusion.10
  163.3 0.1 multiply_convert_fusion.8
  163.4 418.8 %collective-permute-start = (bf16[2,1024]{1,0:T(2,128)(2,1)S(1)}, bf16[2,1024]{1,0:T(2,128)(2,1)S(1)}, u32[]{:S(2)}, u32[]{:S(2)}) collective-permute-start(bf16[2,1024]{1,0:T(2,128)(2,1)S(1)} %slice.146), channel_id=1, source_target_pairs={{0,1},{1,2},{2,3},{3,4},{4,5},{5,6},{6,7},{7,8},{8,9},{9,10},{10,1... | collective-permute-start | bytes 12296 | tf_op jit(solution)/shard_map/ppermute | solution.py:14
  582.2 1.1 slice_convert_fusion
  583.3 0.8 slice_reduce_fusion.2
  584.0 0.1 maximum_convert_fusion
  584.1 1.1 multiply_convert_fusion.7
  585.3 2.2 multiply_reduce_fusion.5
  587.5 0.1 multiply_convert_fusion.6
  587.6 7.9 slice.156
  595.6 6.5 fusion.2
  602.0 17.4 %reshape.100 = bf16[4608,1024]{1,0:T(8,128)(2,1)} reshape(bf16[1024,4608]{1,0:T(8,128)(2,1)} %slice.156) | data formatting | bytes 18874368 | tf_op jit(solution)/shard_map/reshape | solution.py:84
  619.5 7.0 convolution_bitcast_fusion
  626.5 5.8 multiply_convert_fusion.1
  632.4 7.6 fusion
  640.0 5.9 multiply_reduce_fusion.3
  646.0 0.2 multiply_subtract_fusion
  646.2 2.5 fusion.13
  648.8 2.7 fusion.34
  651.5 0.3 multiply_reduce_fusion
  651.8 0.2 broadcast_multiply_fusion
  651.9 1.5 collective-permute-start.2
  653.5 0.1 pad_add_fusion
  653.6 3.3 collective-permute-done.2
  656.9 0.2 multiply_convert_fusion.5
  657.0 5.9 fusion.31
  662.9 6.5 fusion.32
  669.4 0.2 copy.46
  669.7 11.7 select_maximum_fusion
  681.4 0.0 reduce-scatter.5.cloned.1.call-start
  681.4 7.9 fusion.45
  689.3 21.6 %reshape.101 = f32[1024,4608]{1,0:T(8,128)} reshape(f32[4608,1024]{1,0:T(8,128)} %fusion.45) | data formatting | bytes 37748736 | tf_op jit(solution)/shard_map/reshape | solution.py:132
  710.9 9.3 fusion.43
  720.2 7.9 fusion.44
  728.1 37.7 %pad_maximum_fusion = f32[1024,13824]{1,0:T(8,128)} fusion(f32[1024,4608]{1,0:T(8,128)} %reshape.101, f32[1024,4608]{1,0:T(8,128)} %fusion.44, f32[1024,4608]{1,0:T(8,128)} %fusion.43), kind=kLoop, calls=%fused_computation | loop fusion | flops 28311552 | bytes 113246208 | tf_op jit(solution)/shard_map/concatenate | solution.py:49
  765.8 5.9 fusion.23
  771.7 1.0 fusion.28
  772.7 591.5 %reduce-scatter.3.cloned.1.call-done = f32[8,4352]{1,0:T(8,128)} async-done(((f32[1024,4352]{1,0:T(8,128)}), f32[8,4352]{1,0:T(8,128)}) %reduce-scatter.3.cloned.1.call-update) | async-done | bytes 139280 | tf_op jit(solution)/shard_map/reduce_scatter | solution.py:51
  1364.2 0.8 slice.160
  1365.0 1.4 slice.161
  1366.3 1.5 slice.159
  1367.9 0.7 copy.48
  1368.5 1.5 slice_reduce_fusion.3
  1370.0 317.2 %reduce-scatter.5.cloned.1.call-done = f32[8,13824]{1,0:T(8,128)} async-done(((f32[1024,13824]{1,0:T(8,128)}), f32[8,13824]{1,0:T(8,128)}) %reduce-scatter.5.cloned.1.call-update) | async-done | bytes 442384 | tf_op jit(solution)/shard_map/reduce_scatter | solution.py:51
  1687.3 1.8 fusion.42
  1689.0 0.7 reshape.102
  (51 shorter events, 0.2 us)
Async XLA Ops:
  12.8 11.6 copy-start.13
  12.8 11.7 copy-start.14
  12.8 11.8 copy-start.15
  12.8 118.0 %all-to-all-start = ((bf16[128,8,4352]{2,1,0:T(8,128)(2,1)}), bf16[128,8,4352]{2,1,0:T(8,128)(2,1)}, u32[]{:S(2)}, u32[]{:S(2)}) async-start(bf16[128,8,4352]{2,1,0:T(8,128)(2,1)} %stack.10), calls=%async_computation | async-start | bytes 17825792 | tf_op jit(solution)/shard_map/all_to_all | solution.py:35
  140.4 15.4 copy-start.16
  140.4 16.8 copy-start.3
  140.4 447.2 %all-to-all-start.1 = ((bf16[128,8,13824]{2,1,0:T(8,128)(2,1)}), bf16[128,8,13824]{2,1,0:T(8,128)(2,1)}, u32[]{:S(2)}, u32[]{:S(2)}) async-start(bf16[128,8,13824]{2,1,0:T(8,128)(2,1)} %stack.11), calls=%async_computation.1 | async-start | bytes 56623104 | tf_op jit(solution)/shard_map/all_to_all | solution.py:35
  155.7 1208.5 %reduce-scatter.3.cloned.1.call-start = ((), (), s32[]{:S(2)}) async-start(), calls=%async_computation.4 | async-start | bytes 17965056 | tf_op jit(solution)/shard_map/reduce_scatter | solution.py:51
  155.9 2.1 collective-permute-start.1
  163.3 420.8 %copy-start = (f32[128,3072]{1,0:T(8,128)}, f32[128,3072]{1,0:T(8,128)S(1)}, u32[]{:S(2)}) copy-start(f32[128,3072]{1,0:T(8,128)S(1)} %fusion.10) | copy-start | bytes 4718596
  163.4 420.6 %collective-permute-start = (bf16[2,1024]{1,0:T(2,128)(2,1)S(1)}, bf16[2,1024]{1,0:T(2,128)(2,1)S(1)}, u32[]{:S(2)}, u32[]{:S(2)}) collective-permute-start(bf16[2,1024]{1,0:T(2,128)(2,1)S(1)} %slice.146), channel_id=1, source_target_pairs={{0,1},{1,2},{2,3},{3,4},{4,5},{5,6},{6,7},{7,8},{8,9},{9,10},{10,1... | collective-permute-start | bytes 12296 | tf_op jit(solution)/shard_map/ppermute | solution.py:14
  585.2 10.3 copy-start.10
  602.0 17.4 %copy-start.2 = (bf16[128,1024]{1,0:T(8,128)(2,1)S(1)}, bf16[128,1024]{1,0:T(8,128)(2,1)}, u32[]{:S(2)}) copy-start(bf16[128,1024]{1,0:T(8,128)(2,1)} %param.21) | copy-start | bytes 786436
  619.5 7.0 copy-start.18
  632.4 7.6 copy-start.7
  632.4 7.6 copy-start.9
  640.0 8.7 copy-start.11
  645.9 5.5 copy-start.1
  646.0 5.5 copy-start.6
  651.5 5.6 copy-start.4
  651.9 4.9 collective-permute-start.2
  681.4 1005.9 %reduce-scatter.5.cloned.1.call-start = ((), (), s32[]{:S(2)}) async-start(), calls=%async_computation.5 | async-start | bytes 57065472 | tf_op jit(solution)/shard_map/reduce_scatter | solution.py:51
  710.9 9.3 copy-start.8
  765.8 5.9 copy-start.5
  765.8 5.9 copy-start.12
  765.8 5.9 copy-start.17
Sparse Core Ops, SparseCore 0:
  681.5 682.6 reduce-scatter.2
  1370.6 316.5 reduce-scatter.4
